TPU v7x, 256 devices: a whole 4x4x8 slice. The times are simulated.
256 devices in a mesh: seq: 16 (over y_lo, z), chan: 16 (over y_hi, x, core).
Axes of the slice: x: 4, y: 4 (y_hi: 2, y_lo: 2; y = y_hi * 2 + y_lo), z: 8, core: 2. Of those that a mesh axis runs over, the one named last changes fastest.
Arguments:
- tokens: bfloat16 [8192, 8192], P('seq', 'chan'), may hold values from -6 to 6
- norm_gain: float32 [8192], replicated, may hold values from 0.1 to 1.9
- w_in: bfloat16 [8192, 3, 4096], P('seq', None, 'chan'), may hold values from -0.0625 to 0.0625
- short_taps: float32 [3, 3, 4096], P(None, None, 'chan'), may hold values from -3.6 to 3.6
- medium_taps: float32 [128, 256], P(None, 'chan'), may hold values from -0.75 to 0.75
- skip_gain: float32 [4096], P('chan'), may hold values from 0.5 to 1.5
- w_out: bfloat16 [4096, 8192], P('chan'), may hold values from -0.09375 to 0.09375
Outputs:
- block_out: bfloat16 [8192, 8192], P('seq', 'chan')
All inputs are finite; a program needn't handle non-finite values.
Results may differ from a plain program's by a relative error of at most 0.019.
Values may be sent and summed in bfloat16 or wider, within the bound.
A program may use at most 128 MiB of HBM per device.

v0:
```python
import jax
import jax.numpy as jnp
from jax import lax
from jax.sharding import PartitionSpec as P

TAPS = 128
GROUP = 16
EPSILON = 1e-06


def passed_along(value, axis, steps):
    count = lax.axis_size(axis)
    first, last = (max(0, -steps), min(count, count - steps))
    return lax.ppermute(value, axis, [(source, source + steps) for source in range(first, last)])


def short_filter(extended, taps):
    return taps[0] * extended[2:] + taps[1] * extended[1:-1] + taps[2] * extended[:-2]


def per_device(tokens, norm_gain, w_in, short_taps, medium_taps, skip_gain, w_out):
    row_count = tokens.shape[0]
    channels = w_in.shape[2]
    gathered = lax.all_gather(tokens, "chan", axis=1, tiled=True)
    widened = gathered.astype(jnp.float32)
    mean_square = jnp.mean(widened * widened, axis=1, keepdims=True)
    normed = (widened * lax.rsqrt(mean_square + EPSILON) * norm_gain).astype(jnp.bfloat16)
    section = lax.all_gather(w_in, "seq", axis=0, tiled=True)
    flat_section = section.reshape(section.shape[0], 3 * channels)
    summed = jnp.dot(normed, flat_section, preferred_element_type=jnp.float32)
    projected = summed.astype(jnp.bfloat16).reshape(row_count, 3, channels)
    edge_rows = passed_along(projected[row_count - 2 :], "seq", 1)
    extended = lax.optimization_barrier(jnp.concatenate([edge_rows, projected], 0)).astype(
        jnp.float32
    )
    filtered = short_filter(extended, short_taps)
    queries = filtered[:, 0]
    product = (filtered[:, 1] * filtered[:, 2]).astype(jnp.bfloat16)
    product_rows = passed_along(product[row_count - (TAPS - 1) :], "seq", 1)
    reached = jnp.concatenate([product_rows, product], 0)
    floats = lax.optimization_barrier(reached).astype(jnp.float32)
    padded = jnp.concatenate([jnp.zeros((1, channels), jnp.float32), floats], 0)
    block_count = row_count // TAPS
    blocks = padded.reshape(block_count + 1, TAPS, channels)
    windows = jnp.concatenate([blocks[:-1], blocks[1:]], 1)
    cube_shape = (TAPS, TAPS, 2 * TAPS)
    lagged = (
        lax.broadcasted_iota(jnp.int32, cube_shape, 1)
        + TAPS
        - lax.broadcasted_iota(jnp.int32, cube_shape, 2)
    )
    onehot = (lagged == lax.broadcasted_iota(jnp.int32, cube_shape, 0)).astype(jnp.float32)
    toeplitz = jnp.einsum("jg,jis->gis", medium_taps, onehot, precision=lax.Precision.HIGHEST)
    filters = medium_taps.shape[1]
    grouped = windows.reshape(block_count, 2 * TAPS, filters, GROUP)
    convolved = jnp.einsum("gis,bsgc->bigc", toeplitz, grouped, precision=lax.Precision.HIGHEST)
    mixing = skip_gain * floats[TAPS - 1 :] + convolved.reshape(row_count, channels)
    gating = (queries * mixing).astype(jnp.bfloat16)
    partial_out = jnp.dot(gating, w_out, preferred_element_type=jnp.float32)
    rounded_out = lax.optimization_barrier(partial_out.astype(jnp.bfloat16)).astype(jnp.float32)
    projected_out = lax.psum_scatter(
        rounded_out.astype(jnp.bfloat16), "chan", scatter_dimension=1, tiled=True
    ).astype(jnp.float32)
    return (tokens.astype(jnp.float32) + projected_out).astype(jnp.bfloat16)


def solution(mesh):
    in_specs = (
        P("seq", "chan"),
        P(),
        P("seq", None, "chan"),
        P(None, None, "chan"),
        P(None, "chan"),
        P("chan"),
        P("chan", None),
    )
    out_specs = P("seq", "chan")
    return jax.shard_map(
        per_device, mesh=mesh, in_specs=in_specs, out_specs=out_specs, check_vma=False
    )
```

profile of v0, /device:TPU:2, one launch (start us, length us, event | category | flops | bytes accessed | tf_op | source)
XLA Modules:
  0.0 403.7 jit_solution(17343954570505300916)
XLA Ops:
  6.5 0.7 all-gather.3.cloned.1.call-update
  7.3 2.3 copy.10
  9.7 2.6 iota_compare_fusion
  12.3 9.2 %fusion.3 = f32[128,256,16]{1,2,0:T(8,128)} fusion(pred[128,128,256]{2,1,0:T(32,128)(4,1)S(1)} %iota_compare_fusion, f32[128,16]{0,1:T(8,128)S(1)} %copy-done), kind=kOutput, calls=%fused_computation.6 | convolution fusion | flops 805306368 | bytes 6299648 | tf_op jit(solution)/shard_map/jg,jis->gis/dot_general | solution.py:53
  21.5 76.3 %all-gather.3.cloned.1.call-done = bf16[512,8192]{1,0:T(8,128)(2,1)} async-done(((bf16[512,512]{1,0:T(8,128)(2,1)}), bf16[512,8192]{1,0:T(8,128)(2,1)}) %all-gather.3.cloned.1.call-update) | async-done | bytes 8388624 | tf_op jit(solution)/shard_map/all_gather | solution.py:24
  97.8 5.1 %fusion = f32[512]{0:T(512)S(1)} fusion(bf16[512,8192]{1,0:T(8,128)(2,1)} %all-gather.3.cloned.1.call-done), kind=kLoop, calls=%fused_computation.2 | loop fusion | flops 12582400 | bytes 8390656 | tf_op jit(solution)/shard_map/reduce_sum | solution.py:26
  102.9 138.7 %all-gather.5.cloned.1.call-done = bf16[8192,3,256]{0,2,1:T(8,128)(2,1)} async-done(((bf16[512,3,256]{0,2,1:T(8,128)(2,1)}), bf16[8192,3,256]{0,2,1:T(8,128)(2,1)}) %all-gather.5.cloned.1.call-update) | async-done | bytes 12582928 | tf_op jit(solution)/shard_map/all_gather | solution.py:28
  241.6 13.1 %fusion.14 = bf16[512,768]{1,0:T(8,128)(2,1)S(1)} fusion(bf16[8192,768]{0,1:T(8,128)(2,1)} %bitcast.50, bf16[512,8192]{1,0:T(8,128)(2,1)} %all-gather.3.cloned.1.call-done, f32[8192]{0:T(1024)S(1)} %copy-done.5, f32[512]{0:T(512)S(1)} %add_rsqrt_fusion), kind=kOutput, calls=%fused_computation.20 | convolution fusion | flops 6459621376 | bytes 21792768 | tf_op jit(solution)/shard_map/dot_general | solution.py:30
  254.8 1.3 collective-permute-start
  256.1 0.3 copy.11
  256.4 1.0 collective-permute-done
  257.4 0.2 copy.12
  257.6 0.5 pad_maximum_fusion
  258.1 0.1 convert_element_type.43
  258.2 1.4 fusion.12
  259.6 0.1 fusion.25
  259.7 0.1 slice_bitcast_fusion.1
  259.8 4.4 %collective-permute-start.1 = (bf16[127,256]{0,1:T(8,128)(2,1)S(1)}, bf16[127,256]{0,1:T(8,128)(2,1)S(1)}, u32[]{:S(2)}, u32[]{:S(2)}) collective-permute-start(bf16[127,256]{0,1:T(8,128)(2,1)S(1)} %slice_bitcast_fusion.1), channel_id=1, source_target_pairs={{0,16},{16,32},{32,48},{48,64},{64,80},{80,96},{96,112},{112,128},... | collective-permute-start | bytes 195080 | tf_op jit(solution)/shard_map/ppermute | solution.py:14
  264.2 0.1 fusion.33
  264.3 1.6 collective-permute-done.1
  265.8 0.2 pad_maximum_fusion.1
  266.1 0.1 slice.72
  266.2 0.2 pad_slice_fusion
  266.4 1.0 concatenate.20
  267.4 1.1 copy.15
  268.5 1.0 concatenate.21
  269.4 1.2 copy.16
  270.7 5.2 %fusion.17 = f32[4,128,16,16]{1,3,0,2:T(8,128)S(1)} fusion(f32[128,256,16]{1,2,0:T(8,128)} %fusion.3, f32[4,128,16,16]{1,3,0,2:T(8,128)S(1)} %copy.16, f32[4,128,16,16]{1,3,0,2:T(8,128)S(1)} %copy.15), kind=kOutput, calls=%fused_computation.21 | convolution fusion | flops 402915328 | bytes 3670016 | tf_op jit(solution)/shard_map/gis,bsgc->bigc/dot_general | solution.py:56
  275.8 0.2 copy.17
  276.1 5.9 %convolution_convert_fusion = bf16[512,8192]{1,0:T(8,128)(2,1)} fusion(bf16[256,8192]{1,0:T(8,128)(2,1)S(1)} %copy-done.1, f32[32,8,4,128]{3,2,1,0:T(4,128)S(1)} %bitcast.49, f32[512,3,256]{0,2,1:T(8,128)S(1)} %fusion.12, f32[256]{0:T(256)S(1)} %copy-done.3, f32[639,256]{0,1:T(8,128)S(1)} %convert_element_type.46), kind=kOutput, calls=%fused_computation.8 | convolution fusion | flops 2152202240 | bytes 14156800 | tf_op jit(solution)/shard_map/dot_general | solution.py:59
  282.0 113.2 %reduce-scatter.2.cloned.1.call-done = bf16[512,512]{1,0:T(8,128)(2,1)} async-done(((bf16[512,8192]{1,0:T(8,128)(2,1)}), bf16[512,512]{1,0:T(8,128)(2,1)}) %reduce-scatter.2.cloned.1.call-update) | async-done | bytes 524304 | tf_op jit(solution)/shard_map/reduce_scatter | solution.py:61
  395.2 2.0 add_convert_fusion
  (23 shorter events, 0.2 us)
Async XLA Ops:
  6.5 5.8 %copy-start = (f32[128,16]{0,1:T(8,128)S(1)}, f32[128,16]{0,1:T(8,128)}, u32[]{:S(2)}) copy-start(f32[128,16]{0,1:T(8,128)} %param.11) | copy-start | bytes 24580
  6.5 91.3 %all-gather.3.cloned.1.call-start = ((), (), s32[]{:S(2)}) async-start(), calls=%async_computation.1 | async-start | bytes 8912896 | tf_op jit(solution)/shard_map/all_gather | solution.py:24
  7.3 234.3 %all-gather.5.cloned.1.call-start = ((), (), s32[]{:S(2)}) async-start(), calls=%async_computation.2 | async-start | bytes 13369344 | tf_op jit(solution)/shard_map/all_gather | solution.py:28
  9.6 385.6 %reduce-scatter.2.cloned.1.call-start = ((), (), s32[]{:S(2)}) async-start(), calls=%async_computation.3 | async-start | bytes 8912896 | tf_op jit(solution)/shard_map/reduce_scatter | solution.py:61
  21.5 220.1 %copy-start.5 = (f32[8192]{0:T(1024)S(1)}, f32[8192]{0:T(1024)}, u32[]{:S(2)}) copy-start(f32[8192]{0:T(1024)} %param.8) | copy-start | bytes 98308
  241.6 14.5 %copy-start.4 = (f32[3,3,256]{2,1,0:T(4,128)S(1)}, f32[3,3,256]{2,1,0:T(4,128)}, u32[]{:S(2)}) copy-start(f32[3,3,256]{2,1,0:T(4,128)} %param.10) | copy-start | bytes 27652
  254.8 2.6 collective-permute-start
  259.8 6.1 %collective-permute-start.1 = (bf16[127,256]{0,1:T(8,128)(2,1)S(1)}, bf16[127,256]{0,1:T(8,128)(2,1)S(1)}, u32[]{:S(2)}, u32[]{:S(2)}) collective-permute-start(bf16[127,256]{0,1:T(8,128)(2,1)S(1)} %slice_bitcast_fusion.1), channel_id=1, source_target_pairs={{0,16},{16,32},{32,48},{48,64},{64,80},{80,96},{96,112},{112,128},... | collective-permute-start | bytes 195080 | tf_op jit(solution)/shard_map/ppermute | solution.py:14
  267.4 8.7 %copy-start.3 = (f32[256]{0:T(256)S(1)}, f32[256]{0:T(256)}, u32[]{:S(2)}) copy-start(f32[256]{0:T(256)} %param.12) | copy-start | bytes 3076
  269.4 6.6 %copy-start.1 = (bf16[256,8192]{1,0:T(8,128)(2,1)S(1)}, bf16[256,8192]{1,0:T(8,128)(2,1)}, u32[]{:S(2)}) copy-start(bf16[256,8192]{1,0:T(8,128)(2,1)} %param.13) | copy-start | bytes 12582916
  282.0 113.2 %copy-start.2 = (bf16[512,512]{1,0:T(8,128)(2,1)S(1)}, bf16[512,512]{1,0:T(8,128)(2,1)}, u32[]{:S(2)}) copy-start(bf16[512,512]{1,0:T(8,128)(2,1)} %param.7) | copy-start | bytes 1572868
Sparse Core Ops, SparseCore 0:
  9.9 87.8 all-gather.2
  99.6 141.9 all-gather.4
  282.2 113.0 reduce-scatter.1
where the time goes:
time: 404 us
  waiting for transfers between devices  332 us (82%)
  matrix products  33.4 us (8%)
  between operations  13.3 us (3%)
  other arithmetic  12 us (3%)
  local copies, waits for them, and re-layouts  7.71 us (2%)
  starting transfers between devices  5.78 us (1%)
    all_gather x1, waiting for transfers between devices, per_device(): section = lax.all_gather(w_in, 'seq', axis=0, tiled=True)  139 us
    reduce_scatter x1, waiting for transfers between devices, per_device(): lax.psum_scatter(rounded_out.astype(jnp.bfloat16), 'chan', scatter_dimens...  113 us
    all_gather x1, waiting for transfers between devices, per_device(): gathered = lax.all_gather(tokens, 'chan', axis=1, tiled=True)  76.3 us
    dot_general x1, matrix products, per_device(): summed = jnp.dot(normed, flat_section, preferred_element_type=jnp.float32)  13.1 us
    dot_general x1, matrix products, per_device(): jnp.einsum('jg,jis->gis', medium_taps, onehot, precision=lax.Precision.HI...  9.22 us
  transfers between devices with their start and end apart: 5, of which 5 were waited for; matrix products, arithmetic and copies ran while one was open for 5% of the time, Pallas kernels for 0%

commit v1 on v0

--- a/solution.py
+++ b/solution.py
@@ -1,11 +1,22 @@
+import functools
 import jax
 import jax.numpy as jnp
 from jax import lax
 from jax.sharding import PartitionSpec as P
+from jax.lax import all_to_all, axis_size
 
 TAPS = 128
 GROUP = 16
 EPSILON = 1e-06
+
+
+def bring_leaves_on(buf, a_name):
+    now = jnp.stack([buf] * axis_size(a_name), axis=0)
+    mid_arr = jnp.concatenate(all_to_all(now, a_name, 0, 0), 1)
+    return mid_arr
+
+
+assign_indices = functools.partial(bring_leaves_on, a_name="chan")
 
 
 def passed_along(value, axis, steps):
@@ -21,7 +32,7 @@
 def per_device(tokens, norm_gain, w_in, short_taps, medium_taps, skip_gain, w_out):
     row_count = tokens.shape[0]
     channels = w_in.shape[2]
-    gathered = lax.all_gather(tokens, "chan", axis=1, tiled=True)
+    gathered = assign_indices(tokens)
     widened = gathered.astype(jnp.float32)
     mean_square = jnp.mean(widened * widened, axis=1, keepdims=True)
     normed = (widened * lax.rsqrt(mean_square + EPSILON) * norm_gain).astype(jnp.bfloat16)

time: 404 us -> 416 us (1.030)
  waiting for transfers between devices: 332 us -> 322 us
  other arithmetic: 12 us -> 19.8 us
  starting transfers between devices: 5.78 us -> 13.4 us
  local copies, waits for them, and re-layouts: 7.71 us -> 13.1 us
    all_to_all x0 -> x1, waiting for transfers between devices: none -> 208 us  [bring_leaves_on(): mid_arr = jnp.concatenate(all_to_all(now, a_name, 0, 0), 1)]
    all_gather x1, waiting for transfers between devices: 139 us -> 0.01 us  [per_device(): section = lax.all_gather(w_in, 'seq', axis=0, tiled=True)]
    all_gather x1 -> x0, waiting for transfers between devices: 76.3 us -> none  [per_device(): gathered = lax.all_gather(tokens, 'chan', axis=1, tiled=True)]
    convert_element_type x0 -> x1, other arithmetic: none -> 7.75 us  [per_device(): (widened * lax.rsqrt(mean_square + EPSILON) * norm_gain).astype(jnp.bfloa...]
    all_to_all x0 -> x1, starting transfers between devices: none -> 7.61 us  [bring_leaves_on(): mid_arr = jnp.concatenate(all_to_all(now, a_name, 0, 0), 1)]
  transfers between devices with their start and end apart: 5 -> 5, of which waited for: 5 -> 4; matrix products, arithmetic and copies ran while one was open for 5% -> 7% of each run, Pallas kernels for 0% -> 0%
where the time goes in v1:
time: 416 us; the launch traced here: 415 us
  waiting for transfers between devices  322 us (77%)
  matrix products  33.4 us (8%)
  other arithmetic  19.8 us (5%)
  between operations  13.6 us (3%)
  starting transfers between devices  13.4 us (3%)
  local copies, waits for them, and re-layouts  13.1 us (3%)
    all_to_all x1, waiting for transfers between devices, bring_leaves_on(): mid_arr = jnp.concatenate(all_to_all(now, a_name, 0, 0), 1)  208 us
    reduce_scatter x1, waiting for transfers between devices, per_device(): lax.psum_scatter(rounded_out.astype(jnp.bfloat16), 'chan', scatter_dimens...  112 us
    dot_general x1, matrix products, per_device(): summed = jnp.dot(normed, flat_section, preferred_element_type=jnp.float32)  12.9 us
    dot_general x1, matrix products, per_device(): jnp.einsum('jg,jis->gis', medium_taps, onehot, precision=lax.Precision.HI...  9.4 us
  transfers between devices with their start and end apart: 5, of which 4 were waited for; matrix products, arithmetic and copies ran while one was open for 7% of the time, Pallas kernels for 0%

profile of v1, /device:TPU:2, one launch (start us, length us, event | category | flops | bytes accessed | tf_op | source)
XLA Modules:
  0.0 415.3 jit_solution(8571033909812756365)
XLA Ops:
  6.5 2.3 copy.11
  8.9 1.3 copy.10
  10.1 4.1 stack.2
  14.2 7.6 %all-to-all-start = ((bf16[16,512,512]{1,2,0:T(8,128)(2,1)}), bf16[16,512,512]{1,2,0:T(8,128)(2,1)}, u32[]{:S(2)}, u32[]{:S(2)}) async-start(bf16[16,512,512]{1,2,0:T(8,128)(2,1)} %stack.2), calls=%async_computation | async-start | bytes 16777216 | tf_op jit(solution)/shard_map/all_to_all | solution.py:15
  21.9 2.6 iota_compare_fusion
  24.5 9.4 %fusion.3 = f32[128,256,16]{1,2,0:T(8,128)} fusion(pred[128,128,256]{2,1,0:T(32,128)(4,1)S(1)} %iota_compare_fusion, f32[128,16]{0,1:T(8,128)S(1)} %copy-done), kind=kOutput, calls=%fused_computation.6 | convolution fusion | flops 805306368 | bytes 6299648 | tf_op jit(solution)/shard_map/jg,jis->gis/dot_general | solution.py:64
  33.9 208.0 %all-to-all-done = bf16[16,512,512]{1,2,0:T(8,128)(2,1)} async-done(((bf16[16,512,512]{1,2,0:T(8,128)(2,1)}), bf16[16,512,512]{1,2,0:T(8,128)(2,1)}, u32[]{:S(2)}, u32[]{:S(2)}) %all-to-all-start) | async-done | bytes 8388640 | tf_op jit(solution)/shard_map/all_to_all | solution.py:15
  241.9 5.2 %fusion = f32[512]{0:T(512)S(1)} fusion(bf16[16,512,512]{1,2,0:T(8,128)(2,1)} %all-to-all-done), kind=kLoop, calls=%fused_computation.2 | loop fusion | flops 12582400 | bytes 8390656 | tf_op jit(solution)/shard_map/reduce_sum | solution.py:37
  247.1 7.7 %fusion.2 = bf16[16,512,512]{1,2,0:T(8,128)(2,1)} fusion(bf16[16,512,512]{1,2,0:T(8,128)(2,1)} %all-to-all-done, f32[16,512]{1,0:T(8,128)S(1)} %mul.77, f32[512]{0:T(512)S(1)} %add_rsqrt_fusion), kind=kLoop, calls=%fused_computation.4 | loop fusion | flops 16777216 | bytes 16812032 | tf_op jit(solution)/shard_map/convert_element_type | solution.py:38
  254.8 12.9 %convolution_convert_fusion.1 = bf16[512,768]{1,0:T(8,128)(2,1)S(1)} fusion(bf16[512,8192]{0,1:T(8,128)(2,1)} %bitcast.52, bf16[8192,768]{0,1:T(8,128)(2,1)} %bitcast.55), kind=kOutput, calls=%fused_computation.17 | convolution fusion | flops 6442844160 | bytes 21757952 | tf_op jit(solution)/shard_map/dot_general | solution.py:41
  267.7 1.3 collective-permute-start
  269.1 0.3 copy.12
  269.4 1.0 collective-permute-done
  270.4 0.2 copy.13
  270.5 0.5 pad_maximum_fusion
  271.0 0.1 convert_element_type.54
  271.2 1.4 fusion.8
  272.6 0.1 slice_bitcast_fusion.1
  272.7 4.4 %collective-permute-start.1 = (bf16[127,256]{0,1:T(8,128)(2,1)S(1)}, bf16[127,256]{0,1:T(8,128)(2,1)S(1)}, u32[]{:S(2)}, u32[]{:S(2)}) collective-permute-start(bf16[127,256]{0,1:T(8,128)(2,1)S(1)} %slice_bitcast_fusion.1), channel_id=1, source_target_pairs={{0,16},{16,32},{32,48},{48,64},{64,80},{80,96},{96,112},{112,128},... | collective-permute-start | bytes 195080 | tf_op jit(solution)/shard_map/ppermute | solution.py:25
  277.3 1.5 collective-permute-done.1
  278.8 0.2 pad_maximum_fusion.1
  279.0 0.1 slice.72
  279.2 0.2 pad_slice_fusion
  279.4 1.0 concatenate.20
  280.3 1.1 copy.16
  281.4 1.0 concatenate.21
  282.4 1.2 copy.17
  283.6 5.2 %fusion.10 = f32[4,128,16,16]{1,3,0,2:T(8,128)S(1)} fusion(f32[128,256,16]{1,2,0:T(8,128)} %fusion.3, f32[4,128,16,16]{1,3,0,2:T(8,128)S(1)} %copy.17, f32[4,128,16,16]{1,3,0,2:T(8,128)S(1)} %copy.16), kind=kOutput, calls=%fused_computation.18 | convolution fusion | flops 402915328 | bytes 3670016 | tf_op jit(solution)/shard_map/gis,bsgc->bigc/dot_general | solution.py:67
  288.8 0.2 copy.18
  289.0 5.9 %convolution_convert_fusion = bf16[512,8192]{1,0:T(8,128)(2,1)} fusion(bf16[256,8192]{1,0:T(8,128)(2,1)S(1)} %copy-done.2, f32[32,8,4,128]{3,2,1,0:T(4,128)S(1)} %bitcast.54, f32[512,3,256]{0,2,1:T(8,128)S(1)} %fusion.8, f32[256]{0:T(256)S(1)} %copy-done.5, f32[639,256]{0,1:T(8,128)S(1)} %convert_element_type.57), kind=kOutput, calls=%fused_computation.8 | convolution fusion | flops 2152202240 | bytes 14156800 | tf_op jit(solution)/shard_map/dot_general | solution.py:70
  295.0 111.5 %reduce-scatter.2.cloned.1.call-done = bf16[512,512]{1,0:T(8,128)(2,1)} async-done(((bf16[512,8192]{1,0:T(8,128)(2,1)}), bf16[512,512]{1,0:T(8,128)(2,1)}) %reduce-scatter.2.cloned.1.call-update) | async-done | bytes 524304 | tf_op jit(solution)/shard_map/reduce_scatter | solution.py:72
  406.5 2.0 add_convert_fusion
  (28 shorter events, 0.3 us)
Async XLA Ops:
  6.5 18.0 %copy-start = (f32[128,16]{0,1:T(8,128)S(1)}, f32[128,16]{0,1:T(8,128)}, u32[]{:S(2)}) copy-start(f32[128,16]{0,1:T(8,128)} %param.11) | copy-start | bytes 24580
  6.5 248.3 %all-gather.2.cloned.1.call-start = ((), (), s32[]{:S(2)}) async-start(), calls=%async_computation.2 | async-start | bytes 13369344 | tf_op jit(solution)/shard_map/all_gather | solution.py:39
  14.2 7.7 %copy-start.4 = (f32[8192]{0:T(1024)S(1)}, f32[8192]{0:T(1024)}, u32[]{:S(2)}) copy-start(f32[8192]{0:T(1024)} %param.8) | copy-start | bytes 98308
  14.2 227.7 %all-to-all-start = ((bf16[16,512,512]{1,2,0:T(8,128)(2,1)}), bf16[16,512,512]{1,2,0:T(8,128)(2,1)}, u32[]{:S(2)}, u32[]{:S(2)}) async-start(bf16[16,512,512]{1,2,0:T(8,128)(2,1)} %stack.2), calls=%async_computation | async-start | bytes 16777216 | tf_op jit(solution)/shard_map/all_to_all | solution.py:15
  21.8 384.7 %reduce-scatter.2.cloned.1.call-start = ((), (), s32[]{:S(2)}) async-start(), calls=%async_computation.3 | async-start | bytes 8912896 | tf_op jit(solution)/shard_map/reduce_scatter | solution.py:72
  254.8 14.2 %copy-start.6 = (f32[3,3,256]{2,1,0:T(4,128)S(1)}, f32[3,3,256]{2,1,0:T(4,128)}, u32[]{:S(2)}) copy-start(f32[3,3,256]{2,1,0:T(4,128)} %param.10) | copy-start | bytes 27652
  267.7 2.6 collective-permute-start
  272.7 6.1 %collective-permute-start.1 = (bf16[127,256]{0,1:T(8,128)(2,1)S(1)}, bf16[127,256]{0,1:T(8,128)(2,1)S(1)}, u32[]{:S(2)}, u32[]{:S(2)}) collective-permute-start(bf16[127,256]{0,1:T(8,128)(2,1)S(1)} %slice_bitcast_fusion.1), channel_id=1, source_target_pairs={{0,16},{16,32},{32,48},{48,64},{64,80},{80,96},{96,112},{112,128},... | collective-permute-start | bytes 195080 | tf_op jit(solution)/shard_map/ppermute | solution.py:25
  280.3 8.7 %copy-start.5 = (f32[256]{0:T(256)S(1)}, f32[256]{0:T(256)}, u32[]{:S(2)}) copy-start(f32[256]{0:T(256)} %param.12) | copy-start | bytes 3076
  282.4 6.6 %copy-start.2 = (bf16[256,8192]{1,0:T(8,128)(2,1)S(1)}, bf16[256,8192]{1,0:T(8,128)(2,1)}, u32[]{:S(2)}) copy-start(bf16[256,8192]{1,0:T(8,128)(2,1)} %param.13) | copy-start | bytes 12582916
  295.0 113.5 %copy-start.1 = (f32[128,16]{0,1:T(8,128)S(1)}, f32[128,16]{0,1:T(8,128)}, u32[]{:S(2)}) copy-start(f32[128,16]{0,1:T(8,128)} %param.11) | copy-start | bytes 24580
  295.0 111.6 %copy-start.3 = (bf16[512,512]{1,0:T(8,128)(2,1)S(1)}, bf16[512,512]{1,0:T(8,128)(2,1)}, u32[]{:S(2)}) copy-start(bf16[512,512]{1,0:T(8,128)(2,1)} %param.7) | copy-start | bytes 1572868
Sparse Core Ops, SparseCore 0:
  9.2 210.2 all-gather.1
  295.1 111.3 reduce-scatter.1
